TPU v7x, 32 devices: a whole 2x2x4 slice. The times are simulated.
32 devices in a mesh: groups: 2 (over x), prompt: 8 (over z, y), resp: 2 (over core).
Axes of the slice: x: 2, y: 2, z: 4, core: 2. Of those that a mesh axis runs over, the one named last changes fastest.
Arguments:
- queries: bfloat16 [16, 512, 1024], P(('groups', 'prompt'), 'resp'), parts along dimension 0, may hold values from -4096 to 4096
- grad_out: bfloat16 [16, 512, 1024], P(('groups', 'prompt'), 'resp'), parts along dimension 0, may hold values from -48 to 48
- keys_resp: bfloat16 [16, 512, 128], P(('groups', 'prompt'), 'resp'), parts along dimension 0, may hold values from -6 to 6
- values_resp: bfloat16 [16, 512, 128], P(('groups', 'prompt'), 'resp'), parts along dimension 0, may hold values from -6 to 6
- keys_prefix: bfloat16 [1024, 128], P(('groups', 'prompt')), parts along dimension 0, may hold values from -32 to 32
- values_prefix: bfloat16 [1024, 128], P(('groups', 'prompt')), parts along dimension 0, may hold values from -6 to 6
- lengths: int32 [16], P(('groups', 'prompt')), parts along dimension 0, may hold values from 1 to 512, as said below
- block_plan: int32 [16, 4], P(('groups', 'prompt'), 'resp'), parts along dimension 0, may hold values from 0 to 3, as said below
Outputs:
- query_grads: float32 [16, 512, 1024], P(('groups', 'prompt'), 'resp'), parts along dimension 0
- prefix_keygrad: float32 [1024, 128], P(('groups', 'prompt', 'resp')), parts along dimension 0
- prefix_valgrad: float32 [1024, 128], P(('groups', 'prompt', 'resp')), parts along dimension 0
- reply_keygrad: float32 [16, 512, 128], P(('groups', 'prompt'), 'resp'), parts along dimension 0
- reply_valgrad: float32 [16, 512, 128], P(('groups', 'prompt'), 'resp'), parts along dimension 0
There are 2 independent parts, one for each index of `groups`. A program takes and returns all parts, laid end to end along the dimension named above; each array names one. Nothing has to cross between parts.
Inputs may be any that keep to these rules, and one draw needn't show every extreme that they name: `lengths`: one response has exactly 512 live positions. `block_plan`: each row is a permutation of 0 to 3; for every m, blocks 2 * m and 2 * m + 1 stand in different halves of the row.
All inputs are finite; a program needn't handle non-finite values.
Results may differ from a plain program's by a relative error of at most 0.0029.
Values may be sent and summed in bfloat16 or wider, within the bound.
A program may use at most 64 MiB of HBM per device.

v0:
```python
import jax
import jax.numpy as jnp
from jax import lax
from jax.sharding import PartitionSpec as P

RBLK = 128


def block_terms(
    query_block, grad_block, first_row, length, all_keys, all_values, prefix_len, head_count
):
    row_count = query_block.shape[0]
    head_width = all_keys.shape[1]
    key_count = all_keys.shape[0]
    score_scale = head_width ** (-0.5)
    positions = first_row + jnp.arange(row_count, dtype=jnp.int32)
    key_index = jnp.arange(key_count, dtype=jnp.int32)
    relative = key_index - prefix_len
    visible = (key_index[None, :] < prefix_len) | (relative[None, :] <= positions[:, None]) & (
        relative[None, :] < length
    )
    live_rows = positions < length
    query_heads = query_block.reshape(row_count, head_count, head_width)
    grad_heads = jnp.where(
        live_rows[:, None, None],
        grad_block.reshape(row_count, head_count, head_width),
        jnp.zeros((), jnp.bfloat16),
    )
    half_heads = head_count // 2

    def active_block(unused):
        grad_parts = []
        grad_k = jnp.zeros((key_count, head_width), jnp.float32)
        grad_v = jnp.zeros((key_count, head_width), jnp.float32)
        for group_index in range(2):
            query_part = query_heads[:, group_index * half_heads : (group_index + 1) * half_heads]
            grad_part = grad_heads[:, group_index * half_heads : (group_index + 1) * half_heads]
            scores = (
                jnp.einsum("rhd,kd->rhk", query_part, all_keys, preferred_element_type=jnp.float32)
                * score_scale
            )
            scores = jnp.where(visible[:, None, :], scores, -jnp.inf)
            row_max = jnp.max(scores, -1, keepdims=True)
            exponent = jnp.exp(scores - row_max)
            weights = exponent / jnp.sum(exponent, -1, keepdims=True)
            grad_weight = jnp.einsum(
                "rhd,kd->rhk", grad_part, all_values, preferred_element_type=jnp.float32
            )
            row_inner = jnp.sum(weights * grad_weight, -1, keepdims=True)
            grad_score = (weights * (grad_weight - row_inner)).astype(jnp.bfloat16)
            rounded_weights = weights.astype(jnp.bfloat16)
            grad_query = (
                jnp.einsum("rhk,kd->rhd", grad_score, all_keys, preferred_element_type=jnp.float32)
                * score_scale
            )
            grad_parts.append(grad_query)
            grad_k = (
                grad_k
                + jnp.einsum(
                    "rhk,rhd->kd", grad_score, query_part, preferred_element_type=jnp.float32
                )
                * score_scale
            )
            grad_v = grad_v + jnp.einsum(
                "rhk,rhd->kd", rounded_weights, grad_part, preferred_element_type=jnp.float32
            )
        joined = jnp.concatenate(grad_parts, 1).reshape(row_count, head_count * head_width)
        return (joined, grad_k, grad_v)

    def empty_block(unused):
        return (
            jnp.zeros((row_count, head_count * head_width), jnp.float32),
            jnp.zeros((key_count, head_width), jnp.float32),
            jnp.zeros((key_count, head_width), jnp.float32),
        )

    return lax.cond(first_row < length, active_block, empty_block, 0)


def local(
    queries, grad_out, keys_resp, values_resp, keys_prefix, values_prefix, lengths, block_plan
):
    core_count = lax.axis_size("resp")
    slot_count = queries.shape[1]
    head_width = keys_prefix.shape[1]
    full_width = queries.shape[2]
    head_count = full_width // head_width
    block_count = slot_count // RBLK
    total_blocks = block_count * core_count
    length = lengths[0]
    prefix_keys, prefix_values = (
        lax.all_gather(keys_prefix, "prompt", axis=0, tiled=True),
        lax.all_gather(values_prefix, "prompt", axis=0, tiled=True),
    )
    prefix_len = prefix_keys.shape[0]
    plan_row = block_plan[0]
    query_all, grad_all, reply_keys, reply_values = (
        lax.all_gather(queries, "resp", axis=1, tiled=True),
        lax.all_gather(grad_out, "resp", axis=1, tiled=True),
        lax.all_gather(keys_resp, "resp", axis=1, tiled=True),
        lax.all_gather(values_resp, "resp", axis=1, tiled=True),
    )
    query_work = jnp.take(query_all.reshape(total_blocks, RBLK, full_width), plan_row, axis=0)
    grad_work = jnp.take(grad_all.reshape(total_blocks, RBLK, full_width), plan_row, axis=0)
    starts = plan_row * RBLK
    all_keys = jnp.concatenate([prefix_keys, reply_keys[0]], 0)
    all_values = jnp.concatenate([prefix_values, reply_values[0]], 0)

    def advance(totals, block_item):
        query_block, grad_block, first_row = block_item
        grad_query, grad_k, grad_v = block_terms(
            query_block, grad_block, first_row, length, all_keys, all_values, prefix_len, head_count
        )
        return ((totals[0] + grad_k, totals[1] + grad_v), grad_query)

    zeros = jnp.zeros(all_keys.shape, jnp.float32)
    totals, grad_blocks = lax.scan(advance, (zeros, zeros), (query_work, grad_work, starts))
    local_grads = grad_blocks.reshape(1, slot_count, full_width)
    key_total, value_total = totals
    reply_keygrad, reply_valgrad = (
        lax.psum_scatter(key_total[prefix_len:][None], "resp", scatter_dimension=1, tiled=True),
        lax.psum_scatter(value_total[prefix_len:][None], "resp", scatter_dimension=1, tiled=True),
    )
    prefix_k = key_total[:prefix_len]
    prefix_v = value_total[:prefix_len]
    prefix_keygrad, prefix_valgrad = (
        lax.psum_scatter(prefix_k, ("prompt", "resp"), scatter_dimension=0, tiled=True),
        lax.psum_scatter(prefix_v, ("prompt", "resp"), scatter_dimension=0, tiled=True),
    )
    return (local_grads, prefix_keygrad, prefix_valgrad, reply_keygrad, reply_valgrad)


def solution(mesh):
    placed = (
        P(("groups", "prompt"), "resp", None),
        P(("groups", "prompt"), "resp", None),
        P(("groups", "prompt"), "resp", None),
        P(("groups", "prompt"), "resp", None),
        P(("groups", "prompt"), None),
        P(("groups", "prompt"), None),
        P(("groups", "prompt")),
        P(("groups", "prompt"), "resp"),
    )
    return jax.shard_map(
        local,
        mesh=mesh,
        in_specs=placed,
        out_specs=(
            P(("groups", "prompt"), "resp", None),
            P(("groups", "prompt", "resp"), None),
            P(("groups", "prompt", "resp"), None),
            P(("groups", "prompt"), "resp", None),
            P(("groups", "prompt"), "resp", None),
        ),
        check_vma=False,
    )
```

profile of v0, /device:TPU:0, one launch (start us, length us, event | category | flops | bytes accessed | tf_op | source)
XLA Modules:
  0.0 274.7 jit_solution(17285941282429215589)
XLA Ops:
  8.8 2.2 all_gather.20
  11.0 32.4 %all_gather.19 = bf16[512,128]{1,0:T(8,128)(2,1)S(1)} all-gather(bf16[64,128]{1,0:T(8,128)(2,1)} %param.18), channel_id=1, replica_groups=mesh['groups'=2,'prompt'=8,'resp'=2] {'prompt'}, dimensions={0}, use_global_device_ids=true | all-gather | bytes 147456 | tf_op jit(solution)/shard_map/all_gather | solution.py:92
  43.6 1.9 all_gather.23
  45.5 30.5 %all_gather.22 = bf16[512,128]{1,0:T(8,128)(2,1)S(1)} all-gather(bf16[64,128]{1,0:T(8,128)(2,1)S(1)} %copy-done.2), channel_id=1, replica_groups=mesh['groups'=2,'prompt'=8,'resp'=2] {'prompt'}, dimensions={0}, use_global_device_ids=true | all-gather | bytes 147456 | tf_op jit(solution)/shard_map/all_gather | solution.py:93
  76.8 1.8 gather_fusion.1
  78.6 1.8 gather_fusion
  80.6 1.0 copy.59
  81.6 1.0 copy.57
  82.6 32.2 %while.17 = (s32[]{:T(128)}, f32[1024,128]{1,0:T(8,128)}, f32[1024,128]{1,0:T(8,128)}, f32[2,128,1024]{2,1,0:T(8,128)}, s32[2]{0:T(128)S(1)}, /*index=5*/s32[]{:...) while((s32[]{:T(128)}, f32[1024,128]{1,0:T(8,128)}, ...), condition=%wide.region_9.11_spmd.clone, body=%wide.region_0.10_spmd.clone.sunk | while | flops 1629102464 | bytes 53665412 | solution.py:117
  84.5 19.0 %conditional.3 = (f32[1024,128]{1,0:T(8,128)}, f32[1024,128]{1,0:T(8,128)}, f32[1,128,1024]{1,2,0:T(8,128)S(1)}) conditional(s32[]{:T(128)} %convert_element_type.38, () %tuple.97, (s32[1,1024]{1,0:T(1,128)S(1)}, s32[1,1024]{1,0:T(1,128)S(1)}, s32[1,1024]{1,0:T(1,128)S(1)}, s32[]{:T(128)}, s32[128,1]{0,1:T(1,128)S(1)}, /*index=5*/s32[]{:T(128)}, ...), branch_computations={%region_1.2_spmd, %region_2.9_spmd} | conditional | flops 1628578176 | bytes 40028488 | solution.py:77
  85.2 1.3 compare_bitcast_fusion
  87.4 1.1 constant_dynamic-slice_fusion
  88.7 1.0 fusion.53
  89.7 2.3 convolution_bitcast_fusion
  92.0 1.5 multiply_reduce_fusion
  93.8 1.2 convolution_multiply_fusion
  95.5 1.0 fusion.56
  96.5 3.3 %fusion.6 = f32[1024,128]{1,0:T(8,128)} fusion(f32[1024,128]{1,0:T(8,128)} %convolution_bitcast_fusion, bf16[128,8,128]{2,0,1:T(8,128)(2,1)S(1)} %broadcast_select_fusion, f32[128,4]{0,1:T(4,128)S(1)} %get-tuple-element.383, pred[128,1024]{1,0:T(8,128)(4,1)S(1)} %and_or_fusion, bf16[128,8,128]{0,2,1:T(8,128)(2,1)S(1)} %bitcast.100, ...), kind=kOutput, calls=%fused_computation.20 | convolution fusion | flops 271189504 | bytes 1837056 | tf_op jit(solution)/shard_map/while/body/eval_jaxpr/cond/branch_1_fun/rhk,rhd->kd/dot_general | solution.py:64
  99.8 1.5 multiply_reduce_fusion.1
  101.7 1.3 fusion.5
  103.5 2.4 select_add_fusion.3
  106.2 1.0 copy-done.4
  109.1 1.8 conditional.3
  110.0 0.9 broadcast.91
  110.8 2.7 select_add_fusion.3
  113.8 1.0 copy-done.4
  114.8 1.9 slice_bitcast_fusion.1
  116.7 1.9 slice_bitcast_fusion
  119.8 68.4 %reduce-scatter.5.cloned.1.call-done = f32[32,128]{1,0:T(8,128)} async-done(((f32[512,128]{1,0:T(8,128)}), f32[32,128]{1,0:T(8,128)}) %reduce-scatter.5.cloned.1.call-update) | async-done | bytes 16400 | tf_op jit(solution)/shard_map/reduce_scatter | solution.py:127
  188.1 58.7 %reduce-scatter.7.cloned.1.call-done = f32[32,128]{1,0:T(8,128)} async-done(((f32[512,128]{1,0:T(8,128)}), f32[32,128]{1,0:T(8,128)}) %reduce-scatter.7.cloned.1.call-update) | async-done | bytes 16400 | tf_op jit(solution)/shard_map/reduce_scatter | solution.py:128
  246.9 9.4 %reduce-scatter.9.cloned.1.call-done = f32[1,256,128]{2,1,0:T(8,128)} async-done(((f32[1,512,128]{2,1,0:T(8,128)}), f32[1,256,128]{2,1,0:T(8,128)}) %reduce-scatter.9.cloned.1.call-update) | async-done | bytes 131088 | tf_op jit(solution)/shard_map/reduce_scatter | solution.py:121
  256.3 11.5 %reduce-scatter.11.cloned.1.call-done = f32[1,256,128]{2,1,0:T(8,128)} async-done(((f32[1,512,128]{2,1,0:T(8,128)}), f32[1,256,128]{2,1,0:T(8,128)}) %reduce-scatter.11.cloned.1.call-update) | async-done | bytes 131088 | tf_op jit(solution)/shard_map/reduce_scatter | solution.py:122
  (63 shorter events, 9.9 us)
Async XLA Ops:
  7.2 36.4 %copy-start.1 = (bf16[1,256,128]{2,1,0:T(8,128)(2,1)S(1)}, bf16[1,256,128]{2,1,0:T(8,128)(2,1)}, u32[]{:S(2)}) copy-start(bf16[1,256,128]{2,1,0:T(8,128)(2,1)} %param.17) | copy-start | bytes 196612
  7.2 38.3 %copy-start.2 = (bf16[64,128]{1,0:T(8,128)(2,1)S(1)}, bf16[64,128]{1,0:T(8,128)(2,1)}, u32[]{:S(2)}) copy-start(bf16[64,128]{1,0:T(8,128)(2,1)} %param.19) | copy-start | bytes 49156
  7.2 68.8 %copy-start.5 = (s32[1,2]{1,0:T(1,128)S(1)}, s32[1,2]{1,0:T(1,128)}, u32[]{:S(2)}) copy-start(s32[1,2]{1,0:T(1,128)} %param.21) | copy-start | bytes 28
  7.2 69.6 %all-gather.5.cloned.1.call-start = ((), (), s32[]{:S(2)}) async-start(), calls=%async_computation.5 | async-start | bytes 1572864 | tf_op jit(solution)/shard_map/all_gather | solution.py:99
  7.9 70.7 %all-gather.3.cloned.1.call-start = ((), (), s32[]{:S(2)}) async-start(), calls=%async_computation.4 | async-start | bytes 1572864 | tf_op jit(solution)/shard_map/all_gather | solution.py:98
  8.7 179.4 %reduce-scatter.5.cloned.1.call-start = ((), (), s32[]{:S(2)}) async-start(), calls=%async_computation.6 | async-start | bytes 278528 | tf_op jit(solution)/shard_map/reduce_scatter | solution.py:127
  101.6 1.8 copy-start
  103.5 2.6 copy-start.3
  106.2 1.0 copy-start.4
  110.8 2.9 %copy-start.3 = (f32[2,128,1024]{2,1,0:T(8,128)S(1)}, f32[2,128,1024]{2,1,0:T(8,128)}, u32[]{:S(2)}) copy-start(f32[2,128,1024]{2,1,0:T(8,128)} %get-tuple-element.493) | copy-start | bytes 3145732 | tf_op jit(solution)/shard_map/while
  113.8 1.0 copy-start.4
  116.6 130.2 %reduce-scatter.7.cloned.1.call-start = ((), (), s32[]{:S(2)}) async-start(), calls=%async_computation.7 | async-start | bytes 278528 | tf_op jit(solution)/shard_map/reduce_scatter | solution.py:128
  118.6 137.7 %reduce-scatter.9.cloned.1.call-start = ((), (), s32[]{:S(2)}) async-start(), calls=%async_computation.8 | async-start | bytes 393216 | tf_op jit(solution)/shard_map/reduce_scatter | solution.py:121
  119.2 148.7 %reduce-scatter.11.cloned.1.call-start = ((), (), s32[]{:S(2)}) async-start(), calls=%async_computation.9 | async-start | bytes 393216 | tf_op jit(solution)/shard_map/reduce_scatter | solution.py:122
Sparse Core Ops, SparseCore 0:
  9.5 11.7 all-gather.4
  22.9 10.1 all-gather.2
  116.8 71.3 reduce-scatter.4
  192.1 54.7 reduce-scatter.6
  249.5 6.7 reduce-scatter.8
  258.9 8.8 reduce-scatter.10
where the time goes:
time: 275 us
  waiting for transfers between devices  151 us (55%)
  blocking collectives  67.1 us (24%)
  local copies, waits for them, and re-layouts  16.1 us (6%)
  between operations  14.2 us (5%)
  matrix products  14 us (5%)
  other arithmetic  9.68 us (4%)
  loops' own time  2.86 us (1%)
    reduce_scatter x1, waiting for transfers between devices, local(): lax.psum_scatter(prefix_k, ('prompt', 'resp'), scatter_dimension=0, tiled...  68.4 us
    reduce_scatter x1, waiting for transfers between devices, local(): lax.psum_scatter(prefix_v, ('prompt', 'resp'), scatter_dimension=0, tiled...  58.7 us
    all_gather x1, blocking collectives, local(): lax.all_gather(keys_prefix, 'prompt', axis=0, tiled=True)  32.4 us
    all_gather x1, blocking collectives, local(): lax.all_gather(values_prefix, 'prompt', axis=0, tiled=True)  30.5 us
    reduce_scatter x1, waiting for transfers between devices, local(): lax.psum_scatter(value_total[prefix_len:][None], 'resp', scatter_dimensio...  11.5 us
    reduce_scatter x1, waiting for transfers between devices, local(): lax.psum_scatter(key_total[prefix_len:][None], 'resp', scatter_dimension=...  9.44 us
    dot_general x2, matrix products, active_block(): jnp.einsum('rhk,rhd->kd', rounded_weights, grad_part, preferred_element_t...  5.58 us
  transfers between devices with their start and end apart: 6, of which 4 were waited for; matrix products, arithmetic and copies ran while one was open for 2% of the time, Pallas kernels for 0%

commit v1 on v0

v1 whole, which is shorter than its diff:
```python
import functools
import math

import jax
import jax.numpy as jnp
from jax import lax
from jax.experimental import pallas as pl
from jax.experimental.pallas import tpu as pltpu
from jax.sharding import PartitionSpec as P

RBLK = 128
CHUNK = 256
MESH = pl.DeviceIdType.MESH
F32 = jnp.float32
BF16 = jnp.bfloat16


def remote(src, dst, send_sem, recv_sem, device):
    return pltpu.make_async_remote_copy(
        src_ref=src,
        dst_ref=dst,
        send_sem=send_sem,
        recv_sem=recv_sem,
        device_id=device,
        device_id_type=MESH,
    )


def dot_nt(a, b):
    return lax.dot_general(a, b, (((1,), (1,)), ((), ())), preferred_element_type=F32)


def dot_nn(a, b):
    return lax.dot_general(a, b, (((1,), (0,)), ((), ())), preferred_element_type=F32)


def kernel(
    chips, heads, per_step,
    len_ref, plan_ref, q_hbm, g_hbm, kr_hbm, vr_hbm, kp_hbm, vp_hbm,
    dq_hbm, pk_out, pv_out, rk_out, rv_out,
    raw, sb, wk, kv, kt, pt, dt, dq, tb, rb, s2, r2, rt, rr,
    local_sem, pair_send, pair_recv, gat_send, gat_recv, fwd_send, fwd_recv,
    sum_send, sum_recv, out_send, out_recv,
):
    me = lax.axis_index("prompt")
    core = lax.axis_index("resp")
    partner = {"resp": 1 - core}
    shard = kp_hbm.shape[0]
    half = shard // 2
    prefix_len = chips * shard
    own_keys = kr_hbm.shape[1]
    reply_len = 2 * own_keys
    scale = kv.shape[2] ** (-0.5)
    soft = scale * math.log2(math.e)

    barrier = pltpu.get_barrier_semaphore()
    for k in range(1, chips):
        pl.semaphore_signal(
            barrier, inc=1, device_id={"prompt": lax.rem(me + k, chips)}, device_id_type=MESH
        )
    pl.semaphore_signal(barrier, inc=1, device_id=partner, device_id_type=MESH)

    own_rows = pl.ds(pl.multiple_of(prefix_len + core * own_keys, own_keys), own_keys)
    chip_rows = pl.ds(pl.multiple_of(me * shard, shard), shard)
    loads = [
        pltpu.make_async_copy(kp_hbm, kv.at[0, chip_rows], local_sem.at[0]),
        pltpu.make_async_copy(vp_hbm, kv.at[1, chip_rows], local_sem.at[1]),
        pltpu.make_async_copy(kr_hbm.at[0], kv.at[0, own_rows], local_sem.at[2]),
        pltpu.make_async_copy(vr_hbm.at[0], kv.at[1, own_rows], local_sem.at[3]),
        pltpu.make_async_copy(q_hbm, raw.at[0], local_sem.at[4]),
        pltpu.make_async_copy(g_hbm, raw.at[1], local_sem.at[5]),
    ]
    for load in loads:
        load.start()

    length = len_ref[0]
    first, second = plan_ref[0, 0], plan_ref[0, 1]
    own_block = jnp.where(first // 2 == core, first, second)
    other_block = jnp.where(first // 2 == core, second, first)
    own_local = lax.rem(own_block, 2)
    sent_local = 1 - own_local
    sent_block = 2 * core + sent_local

    loads[0].wait()
    loads[1].wait()
    pl.semaphore_wait(barrier, chips)

    def half_rows(chip):
        return pl.ds(pl.multiple_of(chip * shard + core * half, half), half)

    mine = kv.at[:, half_rows(me)]
    gathers = []
    for k in range(1, chips):
        to = lax.rem(me + k, chips)
        copy = remote(mine, mine, gat_send.at[k], gat_recv.at[me], {"prompt": to})
        copy.start()
        gathers.append(copy)
    loads[2].wait()
    loads[3].wait()
    pair_kv = remote(
        kv.at[:, own_rows], kv.at[:, own_rows], pair_send.at[0], pair_recv.at[0], partner
    )
    pair_kv.start()
    loads[4].wait()
    loads[5].wait()

    def stack(block_local, block, target):
        rows = lax.broadcasted_iota(jnp.int32, (RBLK, 128), 0) + block * RBLK
        live = rows < length
        for h in range(heads):
            lanes = slice(h * 128, (h + 1) * 128)
            place = (h * RBLK) // CHUNK
            inner = slice((h * RBLK) % CHUNK, (h * RBLK) % CHUNK + RBLK)
            target[0, place, inner, :] = raw[0, block_local, :, lanes]
            grads = raw[1, block_local, :, lanes]
            target[1, place, inner, :] = jnp.where(live, grads, jnp.zeros_like(grads))

    stack(sent_local, sent_block, sb)
    pair_q = remote(sb, wk.at[1], pair_send.at[1], pair_recv.at[1], partner)
    pair_q.start()
    stack(own_local, own_block, wk.at[0])

    forwards = []
    for k in range(1, chips):
        source = lax.rem(me + chips - k, chips)
        there = kv.at[:, half_rows(source)]
        remote(there, there, gat_send.at[k], gat_recv.at[source], partner).wait_recv()
        copy = remote(there, there, fwd_send.at[k], fwd_recv.at[k], partner)
        copy.start()
        forwards.append(copy)
    for copy in forwards:
        copy.wait_recv()
    pair_kv.wait_recv()
    kt[...] = kv[0].astype(F32).T.astype(BF16)

    for step in range(2):
        block = own_block if step == 0 else other_block
        if step == 1:
            pair_q.wait_recv()

        def rows_chunk(j, carry):
            lane = lax.broadcasted_iota(jnp.int32, (1, CHUNK), 1)
            limit = jnp.minimum(block * RBLK + lax.rem(lane, RBLK), length - 1)
            scores = dot_nt(kv[0], wk[step, 0, j])
            spot = lax.broadcasted_iota(jnp.int32, (reply_len, CHUNK), 0)
            scores = jnp.concatenate(
                [
                    scores[:prefix_len],
                    jnp.where(spot <= limit, scores[prefix_len:], -jnp.inf),
                ],
                0,
            )
            top = jnp.max(scores, 0, keepdims=True)
            e = jnp.exp2((scores - top) * soft)
            inv = 1.0 / jnp.sum(e, 0, keepdims=True)
            gw = dot_nt(kv[1], wk[step, 1, j])
            weights = e * inv
            inner = jnp.sum(weights * gw, 0, keepdims=True)
            gs = (weights * (gw - inner)).astype(BF16)
            pt[step * per_step + j] = weights.astype(BF16)
            dt[step * per_step + j] = gs
            gq = dot_nn(kt[...], gs) * scale
            dq[step, j] = gq.T
            return carry

        lax.fori_loop(0, per_step, rows_chunk, 0)

    stores = []
    for step in range(2):
        for h in range(heads):
            place = (h * RBLK) // CHUNK
            inner = slice((h * RBLK) % CHUNK, (h * RBLK) % CHUNK + RBLK)
            copy = pltpu.make_async_copy(
                dq.at[step, place, inner, :],
                dq_hbm.at[step, :, pl.ds(h * 128, 128)],
                local_sem.at[6 + step * heads + h],
            )
            copy.start()
            stores.append(copy)

    def totals(start, size):
        rows = slice(start, start + size)
        k_sum = v_sum = None
        for i in range(2 * per_step):
            s, j = i // per_step, i % per_step
            k_part = dot_nn(dt[i, rows, :], wk[s, 0, j])
            v_part = dot_nn(pt[i, rows, :], wk[s, 1, j])
            k_sum = k_part if k_sum is None else k_sum + k_part
            v_sum = v_part if v_sum is None else v_sum + v_part
        return k_sum * scale, v_sum

    per = 256 // shard
    count = chips // per
    sums = []
    for n in range(count):
        k_sum, v_sum = totals(n * 256, 256)
        for which, value in ((0, k_sum), (1, v_sum)):
            value = value.reshape(per, 2, half, 128)
            for c in range(2):
                tb[c, n * per : (n + 1) * per, which] = value[:, c]
        span = pl.ds(n * per, per)
        copy = remote(tb.at[1 - core, span], rb.at[span], sum_send.at[n], sum_recv.at[n], partner)
        copy.start()
        sums.append(copy)

    outs = []

    def send_out(n):
        sums[n].wait_recv()
        span = slice(n * per, (n + 1) * per)
        s2[span] = (tb[core, span] + rb[span]).astype(BF16)
        for i in range(per):
            to = n * per + i

            @pl.when(to != me)
            def _():
                remote(
                    s2.at[to], r2.at[me], out_send.at[to], out_recv.at[me], {"prompt": to}
                ).start()

    for n in range(count - 1):
        send_out(n)
    k_sum, v_sum = totals(prefix_len, reply_len)
    for c in range(2):
        rt[c, 0] = k_sum[c * own_keys : (c + 1) * own_keys]
        rt[c, 1] = v_sum[c * own_keys : (c + 1) * own_keys]
    pair_r = remote(rt.at[1 - core], rr, pair_send.at[2], pair_recv.at[2], partner)
    pair_r.start()
    send_out(count - 1)

    pair_r.wait_recv()
    rk_out[0] = rt[core, 0] + rr[0]
    rv_out[0] = rt[core, 1] + rr[1]

    total = tb[core, me] + rb[me]
    for k in range(1, chips):
        source = lax.rem(me + chips - k, chips)
        remote(
            s2.at[source], r2.at[source], out_send.at[source], out_recv.at[source], partner
        ).wait_recv()
        total = total + r2[source].astype(F32)
    pk_out[...] = total[0]
    pv_out[...] = total[1]

    for k in range(1, chips):
        to = lax.rem(me + k, chips)
        remote(s2.at[to], r2.at[me], out_send.at[to], out_recv.at[me], {"prompt": to}).wait_send()
    for copy in gathers + forwards + sums + [pair_kv, pair_q, pair_r]:
        copy.wait_send()
    for copy in stores:
        copy.wait()


def solution(mesh):
    chips = mesh.shape["prompt"]

    def local(
        queries, grad_out, keys_resp, values_resp, keys_prefix, values_prefix, lengths, block_plan
    ):
        slots, width = queries.shape[1:]
        shard, head = keys_prefix.shape
        heads = width // head
        half = shard // 2
        blocks = slots // RBLK
        own_keys = keys_resp.shape[1]
        keys = chips * shard + 2 * own_keys
        per_step = heads * RBLK // CHUNK
        count = chips // (256 // shard)
        vm = pltpu.VMEM
        dma = pltpu.SemaphoreType.DMA
        any_spec = pl.BlockSpec(memory_space=pl.ANY)
        smem = pl.BlockSpec(memory_space=pltpu.SMEM)
        vmem = pl.BlockSpec(memory_space=pltpu.VMEM)
        dq, pk, pv, rk, rv = pl.pallas_call(
            functools.partial(kernel, chips, heads, per_step),
            out_shape=(
                jax.ShapeDtypeStruct((blocks, RBLK, width), F32),
                jax.ShapeDtypeStruct((half, head), F32),
                jax.ShapeDtypeStruct((half, head), F32),
                jax.ShapeDtypeStruct((1, own_keys, head), F32),
                jax.ShapeDtypeStruct((1, own_keys, head), F32),
            ),
            in_specs=[smem, smem] + [any_spec] * 6,
            out_specs=(any_spec, vmem, vmem, vmem, vmem),
            scratch_shapes=[
                vm((2, blocks, RBLK, width), BF16),
                vm((2, per_step, CHUNK, head), BF16),
                vm((2, 2, per_step, CHUNK, head), BF16),
                vm((2, keys, head), BF16),
                vm((head, keys), BF16),
                vm((2 * per_step, keys, CHUNK), BF16),
                vm((2 * per_step, keys, CHUNK), BF16),
                vm((2, per_step, CHUNK, head), F32),
                vm((2, chips, 2, half, head), F32),
                vm((chips, 2, half, head), F32),
                vm((chips, 2, half, head), BF16),
                vm((chips, 2, half, head), BF16),
                vm((2, 2, own_keys, head), F32),
                vm((2, own_keys, head), F32),
                dma((6 + 2 * heads,)),
                dma((3,)),
                dma((3,)),
                dma((chips,)),
                dma((chips,)),
                dma((chips,)),
                dma((chips,)),
                dma((count,)),
                dma((count,)),
                dma((chips,)),
                dma((chips,)),
            ],
            compiler_params=pltpu.CompilerParams(
                collective_id=0, has_side_effects=True, vmem_limit_bytes=60 * 1024 * 1024
            ),
        )(
            lengths,
            block_plan,
            queries.reshape(blocks, RBLK, width),
            grad_out.reshape(blocks, RBLK, width),
            keys_resp,
            values_resp,
            keys_prefix,
            values_prefix,
        )
        in_order = block_plan[0, 0] // blocks == lax.axis_index("resp")
        dq = jnp.where(in_order, dq, dq[::-1])
        return dq.reshape(1, slots, width), pk, pv, rk, rv

    placed = (
        P(("groups", "prompt"), "resp", None),
        P(("groups", "prompt"), "resp", None),
        P(("groups", "prompt"), "resp", None),
        P(("groups", "prompt"), "resp", None),
        P(("groups", "prompt"), None),
        P(("groups", "prompt"), None),
        P(("groups", "prompt")),
        P(("groups", "prompt"), "resp"),
    )
    return jax.shard_map(
        local,
        mesh=mesh,
        in_specs=placed,
        out_specs=(
            P(("groups", "prompt"), "resp", None),
            P(("groups", "prompt", "resp"), None),
            P(("groups", "prompt", "resp"), None),
            P(("groups", "prompt"), "resp", None),
            P(("groups", "prompt"), "resp", None),
        ),
        check_vma=False,
    )
```

time: 275 us -> 38.6 us (0.14)
  waiting for transfers between devices: 151 us -> 0 us
  blocking collectives: 67.1 us -> 0 us
  Pallas kernels: 0 us -> 30.4 us
  matrix products: 14 us -> 0 us
  between operations: 14.2 us -> 1.48 us
  local copies, waits for them, and re-layouts: 16.1 us -> 3.59 us
  other arithmetic: 9.68 us -> 2.74 us
  loops' own time: 2.86 us -> 0 us
    reduce_scatter x4 -> x0, waiting for transfers between devices: 148 us -> none  [the longest x1 68.4 us: local(): lax.psum_scatter(prefix_k, ('prompt', 'resp'), scatter_dimension=0, tiled...]
    all_gather x4 -> x0, blocking collectives: 67.1 us -> none  [the longest x1 32.4 us: local(): lax.all_gather(keys_prefix, 'prompt', axis=0, tiled=True)]
    pallas_call x0 -> x1, Pallas kernels: none -> 30.4 us  [local(): pl.pallas_call(functools.partial(kernel, chips, heads, per_step), out_sha...]
    dot_general x8 -> x0, matrix products: 12 us -> none  [the longest x2 5.58 us: active_block(): jnp.einsum('rhk,rhd->kd', rounded_weights, grad_part, preferred_element_t...]
    add x2 -> x0, other arithmetic: 5.09 us -> none  [advance(): return ((totals[0] + grad_k, totals[1] + grad_v), grad_query)]
    broadcast_in_dim x3 -> x0, local copies, waits for them, and re-layouts: 3.76 us -> none  [the longest x1 1.88 us: local(): value_total[prefix_len:][None]]
    gather x2 -> x0, local copies, waits for them, and re-layouts: 3.61 us -> none  [the longest x1 1.8 us: local(): jnp.take(grad_all.reshape(total_blocks, RBLK, full_width), plan_row, axis=0)]
    another operation x3 -> x0, loops' own time: 2.86 us -> none  [the longest x1 2.72 us: local(): lax.scan(advance, (zeros, zeros), (query_work, grad_work, starts))]
  transfers between devices with their start and end apart: 6 -> 0, of which waited for: 4 -> 0; matrix products, arithmetic and copies ran while one was open for 2% -> 0% of each run, Pallas kernels for 0% -> 0%
where the time goes in v1:
time: 38.6 us; the launch traced here: 38.2 us
  Pallas kernels  30.4 us (79%)
  local copies, waits for them, and re-layouts  3.59 us (9%)
  other arithmetic  2.74 us (7%)
  between operations  1.48 us (4%)
    pallas_call x1, Pallas kernels, local(): pl.pallas_call(functools.partial(kernel, chips, heads, per_step), out_sha...  30.4 us
    unnamed x14, local copies, waits for them, and re-layouts  3.59 us
    select_n x1, other arithmetic, local(): dq = jnp.where(in_order, dq, dq[::-1])  2.74 us

profile of v1, /device:TPU:0, one launch (start us, length us, event | category | flops | bytes accessed | tf_op | source)
XLA Modules:
  0.0 38.2 jit_solution(15755250019852629813)
XLA Ops:
  1.3 0.0 copy-start.4
  1.3 0.6 %copy-done.4 = s32[1,2]{1,0:T(1,128)S(1)} copy-done((s32[1,2]{1,0:T(1,128)S(1)}, s32[1,2]{1,0:T(1,128)}, u32[]{:S(2)}) %copy-start.4) | copy-done | bytes 32
  2.1 30.4 %shard_map.119 = (f32[2,128,1024]{2,1,0:T(8,128)}, f32[32,128]{1,0:T(8,128)}, f32[32,128]{1,0:T(8,128)}, f32[1,256,128]{2,1,0:T(8,128)}, f32[1,256,128]{2,1,0:T(8,128)}) custom-call(s32[1]{0:T(128)S(6)} %copy.17.len_ref, s32[1,2]{1,0:T(1,128)} %plan_ref.1, bf16[2,128,1024]{2,1,0:T(8,128)(2,1)} %bitcast.6, bf16[2,128,1024]{2,1,0:T(8,128)(2,1)} %bitcast.7, ...), custom_call_target="tpu_custom_call" | custom-call | tf_op jit(solution)/shard_map/pallas_call | solution.py:274
  32.5 0.0 copy-start.3
  32.5 0.0 copy-start.1
  32.5 2.7 %reverse_select_fusion = f32[2,128,1024]{2,1,0:T(8,128)} fusion(f32[2,128,1024]{2,1,0:T(8,128)} %get-tuple-element.10, pred[]{:T(512)S(6)} %eq.3), kind=kLoop, calls=%fused_computation | loop fusion | flops 262144 | bytes 2097153 | tf_op jit(solution)/shard_map/jit(_where)/select_n | solution.py:326
  35.3 0.0 copy-done.3
  35.3 0.0 copy-start.2
  35.3 0.6 %copy.18 = f32[32,128]{1,0:T(8,128)} copy(f32[32,128]{1,0:T(8,128)S(1)} %copy-done.3) | data formatting | bytes 32768
  35.9 0.1 copy-done.2
  36.0 0.6 %copy.19 = f32[32,128]{1,0:T(8,128)} copy(f32[32,128]{1,0:T(8,128)S(1)} %copy-done.2) | data formatting | bytes 32768
  36.6 0.0 copy-done.1
  36.6 0.0 copy-start
  36.6 0.7 %copy.20 = f32[1,256,128]{2,1,0:T(8,128)} copy(f32[1,256,128]{2,1,0:T(8,128)S(1)} %copy-done.1) | data formatting | bytes 262144
  37.3 0.3 copy-done
  37.6 0.7 %copy.21 = f32[1,256,128]{2,1,0:T(8,128)} copy(f32[1,256,128]{2,1,0:T(8,128)S(1)} %copy-done) | data formatting | bytes 262144
Async XLA Ops:
  1.3 0.7 %copy-start.4 = (s32[1,2]{1,0:T(1,128)S(1)}, s32[1,2]{1,0:T(1,128)}, u32[]{:S(2)}) copy-start(s32[1,2]{1,0:T(1,128)} %plan_ref.1) | copy-start | bytes 28
  32.5 2.8 %copy-start.3 = (f32[32,128]{1,0:T(8,128)S(1)}, f32[32,128]{1,0:T(8,128)}, u32[]{:S(2)}) copy-start(f32[32,128]{1,0:T(8,128)} %get-tuple-element.21) | copy-start | bytes 49156
  32.5 4.1 %copy-start.1 = (f32[1,256,128]{2,1,0:T(8,128)S(1)}, f32[1,256,128]{2,1,0:T(8,128)}, u32[]{:S(2)}) copy-start(f32[1,256,128]{2,1,0:T(8,128)} %get-tuple-element.23) | copy-start | bytes 393220
  35.3 0.7 %copy-start.2 = (f32[32,128]{1,0:T(8,128)S(1)}, f32[32,128]{1,0:T(8,128)}, u32[]{:S(2)}) copy-start(f32[32,128]{1,0:T(8,128)} %get-tuple-element.22) | copy-start | bytes 49156
  36.6 1.0 %copy-start = (f32[1,256,128]{2,1,0:T(8,128)S(1)}, f32[1,256,128]{2,1,0:T(8,128)}, u32[]{:S(2)}) copy-start(f32[1,256,128]{2,1,0:T(8,128)} %get-tuple-element.24) | copy-start | bytes 393220

commit v2 on v1

--- a/solution.py
+++ b/solution.py
@@ -37,8 +37,8 @@
 def kernel(
     chips, heads, per_step,
     len_ref, plan_ref, q_hbm, g_hbm, kr_hbm, vr_hbm, kp_hbm, vp_hbm,
-    dq_hbm, pk_out, pv_out, rk_out, rv_out,
-    raw, sb, wk, kv, kt, pt, dt, dq, tb, rb, s2, r2, rt, rr,
+    dq, pk_out, pv_out, rk_out, rv_out,
+    raw, sb, wk, kv, kt, pt, dt, tb, rb, s2, r2, rt, rr,
     local_sem, pair_send, pair_recv, gat_send, gat_recv, fwd_send, fwd_recv,
     sum_send, sum_recv, out_send, out_recv,
 ):
@@ -160,23 +160,13 @@
             pt[step * per_step + j] = weights.astype(BF16)
             dt[step * per_step + j] = gs
             gq = dot_nn(kt[...], gs) * scale
-            dq[step, j] = gq.T
+            gq = gq.T
+            for i in range(CHUNK // RBLK):
+                lanes = pl.multiple_of((j * (CHUNK // RBLK) + i) * 128, 128)
+                dq[step, :, pl.ds(lanes, 128)] = gq[i * RBLK : (i + 1) * RBLK]
             return carry
 
         lax.fori_loop(0, per_step, rows_chunk, 0)
-
-    stores = []
-    for step in range(2):
-        for h in range(heads):
-            place = (h * RBLK) // CHUNK
-            inner = slice((h * RBLK) % CHUNK, (h * RBLK) % CHUNK + RBLK)
-            copy = pltpu.make_async_copy(
-                dq.at[step, place, inner, :],
-                dq_hbm.at[step, :, pl.ds(h * 128, 128)],
-                local_sem.at[6 + step * heads + h],
-            )
-            copy.start()
-            stores.append(copy)
 
     def totals(start, size):
         rows = slice(start, start + size)
@@ -247,7 +237,20 @@
         remote(s2.at[to], r2.at[me], out_send.at[to], out_recv.at[me], {"prompt": to}).wait_send()
     for copy in gathers + forwards + sums + [pair_kv, pair_q, pair_r]:
         copy.wait_send()
-    for copy in stores:
+
+
+def finish(plan_ref, dq, pk, pv, rk, rv, dq_out, pk_out, pv_out, rk_out, rv_out, sem):
+    core = lax.axis_index("resp")
+    copies = []
+    for s in range(dq.shape[0]):
+        step = jnp.where(plan_ref[0, s] // 2 == core, 0, 1)
+        rows = pl.ds(s * RBLK, RBLK)
+        copies.append(pltpu.make_async_copy(dq.at[step], dq_out.at[0, rows], sem.at[s]))
+    for i, (src, dst) in enumerate(((pk, pk_out), (pv, pv_out), (rk, rk_out), (rv, rv_out))):
+        copies.append(pltpu.make_async_copy(src, dst, sem.at[dq.shape[0] + i]))
+    for copy in copies:
+        copy.start()
+    for copy in copies:
         copy.wait()
 
 
@@ -271,17 +274,18 @@
         any_spec = pl.BlockSpec(memory_space=pl.ANY)
         smem = pl.BlockSpec(memory_space=pltpu.SMEM)
         vmem = pl.BlockSpec(memory_space=pltpu.VMEM)
-        dq, pk, pv, rk, rv = pl.pallas_call(
+        shapes = (
+            (blocks, RBLK, width),
+            (half, head),
+            (half, head),
+            (1, own_keys, head),
+            (1, own_keys, head),
+        )
+        parts = pl.pallas_call(
             functools.partial(kernel, chips, heads, per_step),
-            out_shape=(
-                jax.ShapeDtypeStruct((blocks, RBLK, width), F32),
-                jax.ShapeDtypeStruct((half, head), F32),
-                jax.ShapeDtypeStruct((half, head), F32),
-                jax.ShapeDtypeStruct((1, own_keys, head), F32),
-                jax.ShapeDtypeStruct((1, own_keys, head), F32),
-            ),
+            out_shape=tuple(vm(shape, F32) for shape in shapes),
             in_specs=[smem, smem] + [any_spec] * 6,
-            out_specs=(any_spec, vmem, vmem, vmem, vmem),
+            out_specs=(vmem,) * 5,
             scratch_shapes=[
                 vm((2, blocks, RBLK, width), BF16),
                 vm((2, per_step, CHUNK, head), BF16),
@@ -290,14 +294,13 @@
                 vm((head, keys), BF16),
                 vm((2 * per_step, keys, CHUNK), BF16),
                 vm((2 * per_step, keys, CHUNK), BF16),
-                vm((2, per_step, CHUNK, head), F32),
                 vm((2, chips, 2, half, head), F32),
                 vm((chips, 2, half, head), F32),
                 vm((chips, 2, half, head), BF16),
                 vm((chips, 2, half, head), BF16),
                 vm((2, 2, own_keys, head), F32),
                 vm((2, own_keys, head), F32),
-                dma((6 + 2 * heads,)),
+                dma((6,)),
                 dma((3,)),
                 dma((3,)),
                 dma((chips,)),
@@ -322,9 +325,15 @@
             keys_prefix,
             values_prefix,
         )
-        in_order = block_plan[0, 0] // blocks == lax.axis_index("resp")
-        dq = jnp.where(in_order, dq, dq[::-1])
-        return dq.reshape(1, slots, width), pk, pv, rk, rv
+        parts = [pltpu.with_memory_space_constraint(part, pltpu.VMEM) for part in parts]
+        shapes = ((1, slots, width),) + shapes[1:]
+        return pl.pallas_call(
+            finish,
+            out_shape=tuple(jax.ShapeDtypeStruct(shape, F32) for shape in shapes),
+            in_specs=[smem] + [vmem] * 5,
+            out_specs=(any_spec,) * 5,
+            scratch_shapes=[dma((blocks + 4,))],
+        )(block_plan, *parts)
 
     placed = (
         P(("groups", "prompt"), "resp", None),

time: 38.6 us -> 32.9 us (0.85)
  local copies, waits for them, and re-layouts: 3.59 us -> 0 us
  other arithmetic: 2.74 us -> 0 us
  Pallas kernels: 30.4 us -> 31.4 us
    unnamed x14 -> x0, local copies, waits for them, and re-layouts: 3.59 us -> none
    select_n x1 -> x0, other arithmetic: 2.74 us -> none  [local(): dq = jnp.where(in_order, dq, dq[::-1])]
    pallas_call x0 -> x1, Pallas kernels: none -> 1.79 us  [local(): pl.pallas_call(finish, out_shape=tuple((jax.ShapeDtypeStruct(shape, F32)...]
    pallas_call x1, Pallas kernels: 30.4 us -> 29.6 us  [local(): pl.pallas_call(functools.partial(kernel, chips, heads, per_step), out_sha...]
where the time goes in v2:
time: 32.9 us; the launch traced here: 32.7 us
  Pallas kernels  31.4 us (95%)
  between operations  1.29 us (4%)
    pallas_call x1, Pallas kernels, local(): pl.pallas_call(functools.partial(kernel, chips, heads, per_step), out_sha...  29.6 us
    pallas_call x1, Pallas kernels, local(): pl.pallas_call(finish, out_shape=tuple((jax.ShapeDtypeStruct(shape, F32)...  1.79 us

profile of v2, /device:TPU:0, one launch (start us, length us, event | category | flops | bytes accessed | tf_op | source)
XLA Modules:
  0.0 32.7 jit_solution(18159631284771540579)
XLA Ops:
  1.3 29.6 %shard_map.119 = (f32[2,128,1024]{2,1,0:T(8,128)S(1)}, f32[32,128]{1,0:T(8,128)S(1)}, f32[32,128]{1,0:T(8,128)S(1)}, f32[1,256,128]{2,1,0:T(8,128)S(1)}, f32[1,256,128]{2,1,0:T(8,128)S(1)}) custom-call(s32[1]{0:T(128)S(6)} %copy.13.len_ref, s32[1,2]{1,0:T(1,128)} %plan_ref.3, bf16[2,128,1024]{2,1,0:T(8,128)(2,1)} %bitcast.2, bf16[2,128,1024]{2,1,0:T(8,128)(2,1)} %bitcast.3, ...), custom_call_target="tpu_custom_call" | custom-call | tf_op jit(solution)/shard_map/pallas_call | solution.py:284
  30.9 1.8 %shard_map.120 = (f32[1,256,1024]{2,1,0:T(8,128)}, f32[32,128]{1,0:T(8,128)}, f32[32,128]{1,0:T(8,128)}, f32[1,256,128]{2,1,0:T(8,128)}, f32[1,256,128]{2,1,0:T(8,128)}) custom-call(s32[1,2]{1,0:T(1,128)} %plan_ref.3, f32[2,128,1024]{2,1,0:T(8,128)S(1)} %get-tuple-element.10.dq, f32[32,128]{1,0:T(8,128)S(1)} %get-tuple-element.11.pk, ...), custom_call_target="tpu_custom_call" | custom-call | tf_op jit(solution)/shard_map/pallas_call | solution.py:330

commit v3 on v2

--- a/solution.py
+++ b/solution.py
@@ -131,18 +131,22 @@
     for copy in forwards:
         copy.wait_recv()
     pair_kv.wait_recv()
-    kt[...] = kv[0].astype(F32).T.astype(BF16)
-
-    for step in range(2):
-        block = own_block if step == 0 else other_block
-        if step == 1:
-            pair_q.wait_recv()
+
+    pair_q.wait_recv()
+    keys_of = (prefix_len + own_keys, prefix_len + reply_len)
+    low_block = jnp.where(core == 0, own_block, other_block)
+    high_block = jnp.where(core == 0, other_block, own_block)
+    place_of = (core, 1 - core)
+
+    for level, block in ((0, low_block), (1, high_block)):
+        keys = keys_of[level]
+        place = place_of[level]
 
         def rows_chunk(j, carry):
             lane = lax.broadcasted_iota(jnp.int32, (1, CHUNK), 1)
             limit = jnp.minimum(block * RBLK + lax.rem(lane, RBLK), length - 1)
-            scores = dot_nt(kv[0], wk[step, 0, j])
-            spot = lax.broadcasted_iota(jnp.int32, (reply_len, CHUNK), 0)
+            scores = dot_nt(kv[0, :keys], wk[place, 0, j])
+            spot = lax.broadcasted_iota(jnp.int32, (keys - prefix_len, CHUNK), 0)
             scores = jnp.concatenate(
                 [
                     scores[:prefix_len],
@@ -153,37 +157,32 @@
             top = jnp.max(scores, 0, keepdims=True)
             e = jnp.exp2((scores - top) * soft)
             inv = 1.0 / jnp.sum(e, 0, keepdims=True)
-            gw = dot_nt(kv[1], wk[step, 1, j])
+            gw = dot_nt(kv[1, :keys], wk[place, 1, j])
             weights = e * inv
             inner = jnp.sum(weights * gw, 0, keepdims=True)
-            gs = (weights * (gw - inner)).astype(BF16)
-            pt[step * per_step + j] = weights.astype(BF16)
-            dt[step * per_step + j] = gs
-            gq = dot_nn(kt[...], gs) * scale
-            gq = gq.T
-            for i in range(CHUNK // RBLK):
-                lanes = pl.multiple_of((j * (CHUNK // RBLK) + i) * 128, 128)
-                dq[step, :, pl.ds(lanes, 128)] = gq[i * RBLK : (i + 1) * RBLK]
+            pt[level * per_step + j, :keys] = weights.astype(BF16)
+            dt[level * per_step + j, :keys] = (weights * (gw - inner)).astype(BF16)
             return carry
 
         lax.fori_loop(0, per_step, rows_chunk, 0)
 
-    def totals(start, size):
+    def totals(start, size, levels):
         rows = slice(start, start + size)
         k_sum = v_sum = None
-        for i in range(2 * per_step):
-            s, j = i // per_step, i % per_step
-            k_part = dot_nn(dt[i, rows, :], wk[s, 0, j])
-            v_part = dot_nn(pt[i, rows, :], wk[s, 1, j])
-            k_sum = k_part if k_sum is None else k_sum + k_part
-            v_sum = v_part if v_sum is None else v_sum + v_part
+        for level in levels:
+            for j in range(per_step):
+                i = level * per_step + j
+                k_part = dot_nn(dt[i, rows, :], wk[place_of[level], 0, j])
+                v_part = dot_nn(pt[i, rows, :], wk[place_of[level], 1, j])
+                k_sum = k_part if k_sum is None else k_sum + k_part
+                v_sum = v_part if v_sum is None else v_sum + v_part
         return k_sum * scale, v_sum
 
     per = 256 // shard
     count = chips // per
     sums = []
     for n in range(count):
-        k_sum, v_sum = totals(n * 256, 256)
+        k_sum, v_sum = totals(n * 256, 256, (0, 1))
         for which, value in ((0, k_sum), (1, v_sum)):
             value = value.reshape(per, 2, half, 128)
             for c in range(2):
@@ -208,15 +207,30 @@
                     s2.at[to], r2.at[me], out_send.at[to], out_recv.at[me], {"prompt": to}
                 ).start()
 
-    for n in range(count - 1):
-        send_out(n)
-    k_sum, v_sum = totals(prefix_len, reply_len)
     for c in range(2):
-        rt[c, 0] = k_sum[c * own_keys : (c + 1) * own_keys]
-        rt[c, 1] = v_sum[c * own_keys : (c + 1) * own_keys]
+        k_sum, v_sum = totals(prefix_len + c * own_keys, own_keys, (0, 1) if c == 0 else (1,))
+        rt[c, 0] = k_sum
+        rt[c, 1] = v_sum
+        if c < count - 1:
+            send_out(c)
     pair_r = remote(rt.at[1 - core], rr, pair_send.at[2], pair_recv.at[2], partner)
     pair_r.start()
-    send_out(count - 1)
+    for n in range(min(2, count - 1), count):
+        send_out(n)
+
+    kt[...] = kv[0].astype(F32).T.astype(BF16)
+    for level in range(2):
+        keys = keys_of[level]
+        place = place_of[level]
+
+        def grads_chunk(j, carry):
+            gq = (dot_nn(kt[:, :keys], dt[level * per_step + j, :keys]) * scale).T
+            for i in range(CHUNK // RBLK):
+                lanes = pl.multiple_of((j * (CHUNK // RBLK) + i) * 128, 128)
+                dq[place, :, pl.ds(lanes, 128)] = gq[i * RBLK : (i + 1) * RBLK]
+            return carry
+
+        lax.fori_loop(0, per_step, grads_chunk, 0)
 
     pair_r.wait_recv()
     rk_out[0] = rt[core, 0] + rr[0]

time: 32.9 us -> 29.9 us (0.909)
  Pallas kernels: 31.4 us -> 28.3 us
    pallas_call x1, Pallas kernels: 29.6 us -> 26.5 us  [local(): pl.pallas_call(functools.partial(kernel, chips, heads, per_step), out_sha...]
where the time goes in v3:
time: 29.9 us; the launch traced here: 29.6 us
  Pallas kernels  28.3 us (95%)
  between operations  1.29 us (4%)
    pallas_call x1, Pallas kernels, local(): pl.pallas_call(functools.partial(kernel, chips, heads, per_step), out_sha...  26.5 us
    pallas_call x1, Pallas kernels, local(): pl.pallas_call(finish, out_shape=tuple((jax.ShapeDtypeStruct(shape, F32)...  1.79 us

profile of v3, /device:TPU:0, one launch (start us, length us, event | category | flops | bytes accessed | tf_op | source)
XLA Modules:
  0.0 29.6 jit_solution(10703463551757836312)
XLA Ops:
  1.3 26.5 %shard_map.119 = (f32[2,128,1024]{2,1,0:T(8,128)S(1)}, f32[32,128]{1,0:T(8,128)S(1)}, f32[32,128]{1,0:T(8,128)S(1)}, f32[1,256,128]{2,1,0:T(8,128)S(1)}, f32[1,256,128]{2,1,0:T(8,128)S(1)}) custom-call(s32[1]{0:T(128)S(6)} %copy.13.len_ref, s32[1,2]{1,0:T(1,128)} %plan_ref.3, bf16[2,128,1024]{2,1,0:T(8,128)(2,1)} %bitcast.2, bf16[2,128,1024]{2,1,0:T(8,128)(2,1)} %bitcast.3, ...), custom_call_target="tpu_custom_call" | custom-call | tf_op jit(solution)/shard_map/pallas_call | solution.py:298
  27.8 1.8 %shard_map.120 = (f32[1,256,1024]{2,1,0:T(8,128)}, f32[32,128]{1,0:T(8,128)}, f32[32,128]{1,0:T(8,128)}, f32[1,256,128]{2,1,0:T(8,128)}, f32[1,256,128]{2,1,0:T(8,128)}) custom-call(s32[1,2]{1,0:T(1,128)} %plan_ref.3, f32[2,128,1024]{2,1,0:T(8,128)S(1)} %get-tuple-element.10.dq, f32[32,128]{1,0:T(8,128)S(1)} %get-tuple-element.11.pk, ...), custom_call_target="tpu_custom_call" | custom-call | tf_op jit(solution)/shard_map/pallas_call | solution.py:344

commit v4 on v3

--- a/solution.py
+++ b/solution.py
@@ -10,6 +10,7 @@
 
 RBLK = 128
 CHUNK = 256
+HIDDEN = -1e30
 MESH = pl.DeviceIdType.MESH
 F32 = jnp.float32
 BF16 = jnp.bfloat16
@@ -38,7 +39,7 @@
     chips, heads, per_step,
     len_ref, plan_ref, q_hbm, g_hbm, kr_hbm, vr_hbm, kp_hbm, vp_hbm,
     dq, pk_out, pv_out, rk_out, rv_out,
-    raw, sb, wk, kv, kt, pt, dt, tb, rb, s2, r2, rt, rr,
+    raw, sb, wk, kv, kt, pt, dt, pr, dr, er, gr, stat, tb, rb, s2, r2, rt, rr,
     local_sem, pair_send, pair_recv, gat_send, gat_recv, fwd_send, fwd_recv,
     sum_send, sum_recv, out_send, out_recv,
 ):
@@ -81,29 +82,8 @@
     sent_local = 1 - own_local
     sent_block = 2 * core + sent_local
 
-    loads[0].wait()
-    loads[1].wait()
-    pl.semaphore_wait(barrier, chips)
-
-    def half_rows(chip):
-        return pl.ds(pl.multiple_of(chip * shard + core * half, half), half)
-
-    mine = kv.at[:, half_rows(me)]
-    gathers = []
-    for k in range(1, chips):
-        to = lax.rem(me + k, chips)
-        copy = remote(mine, mine, gat_send.at[k], gat_recv.at[me], {"prompt": to})
-        copy.start()
-        gathers.append(copy)
-    loads[2].wait()
-    loads[3].wait()
-    pair_kv = remote(
-        kv.at[:, own_rows], kv.at[:, own_rows], pair_send.at[0], pair_recv.at[0], partner
-    )
-    pair_kv.start()
-    loads[4].wait()
-    loads[5].wait()
-
+    for load in loads[2:]:
+        load.wait()
     def stack(block_local, block, target):
         rows = lax.broadcasted_iota(jnp.int32, (RBLK, 128), 0) + block * RBLK
         live = rows < length
@@ -115,10 +95,58 @@
             grads = raw[1, block_local, :, lanes]
             target[1, place, inner, :] = jnp.where(live, grads, jnp.zeros_like(grads))
 
+    blocks_of = (jnp.where(core == 0, own_block, other_block), jnp.where(core == 0, other_block, own_block))
+    place_of = (core, 1 - core)
+
+    def piece(place, block, part, slot):
+        keys = pl.ds(pl.multiple_of(prefix_len + part * own_keys, own_keys), own_keys)
+
+        def rows_chunk(j, carry):
+            lane = lax.broadcasted_iota(jnp.int32, (1, CHUNK), 1)
+            limit = jnp.minimum(block * RBLK + lax.rem(lane, RBLK), length - 1)
+            spot = lax.broadcasted_iota(jnp.int32, (own_keys, CHUNK), 0) + part * own_keys
+            scores = dot_nt(kv[0, keys], wk[place, 0, j])
+            scores = jnp.where(spot <= limit, scores, HIDDEN)
+            top = jnp.max(scores, 0, keepdims=True)
+            e = jnp.exp2((scores - top) * soft)
+            gw = dot_nt(kv[1, keys], wk[place, 1, j])
+            i = slot * per_step + j
+            er[i] = e
+            gr[i] = gw
+            stat[0, i] = top
+            stat[1, i] = jnp.sum(e, 0, keepdims=True)
+            stat[2, i] = jnp.sum(e * gw, 0, keepdims=True)
+            return carry
+
+        lax.fori_loop(0, per_step, rows_chunk, 0)
+
     stack(sent_local, sent_block, sb)
+    stack(own_local, own_block, wk.at[0])
+    piece(0, own_block, core, 2 * core)
+
+    loads[0].wait()
+    loads[1].wait()
+    pl.semaphore_wait(barrier, chips)
+
+    def half_rows(chip):
+        return pl.ds(pl.multiple_of(chip * shard + core * half, half), half)
+
+    mine = kv.at[:, half_rows(me)]
+    gathers = []
+    for k in range(1, chips):
+        to = lax.rem(me + k, chips)
+        copy = remote(mine, mine, gat_send.at[k], gat_recv.at[me], {"prompt": to})
+        copy.start()
+        gathers.append(copy)
+    pair_kv = remote(
+        kv.at[:, own_rows], kv.at[:, own_rows], pair_send.at[0], pair_recv.at[0], partner
+    )
+    pair_kv.start()
     pair_q = remote(sb, wk.at[1], pair_send.at[1], pair_recv.at[1], partner)
     pair_q.start()
-    stack(own_local, own_block, wk.at[0])
+    pair_kv.wait_recv()
+    pair_q.wait_recv()
+    piece(1 - core, blocks_of[1], 0, 1)
 
     forwards = []
     for k in range(1, chips):
@@ -128,78 +156,82 @@
         copy = remote(there, there, fwd_send.at[k], fwd_recv.at[k], partner)
         copy.start()
         forwards.append(copy)
+
+    piece(1, other_block, 1 - core, 2 * (1 - core))
     for copy in forwards:
         copy.wait_recv()
-    pair_kv.wait_recv()
-
-    pair_q.wait_recv()
-    keys_of = (prefix_len + own_keys, prefix_len + reply_len)
-    low_block = jnp.where(core == 0, own_block, other_block)
-    high_block = jnp.where(core == 0, other_block, own_block)
-    place_of = (core, 1 - core)
-
-    for level, block in ((0, low_block), (1, high_block)):
-        keys = keys_of[level]
+
+    slots_of = ((0,), (1, 2))
+    for level in range(2):
         place = place_of[level]
 
-        def rows_chunk(j, carry):
-            lane = lax.broadcasted_iota(jnp.int32, (1, CHUNK), 1)
-            limit = jnp.minimum(block * RBLK + lax.rem(lane, RBLK), length - 1)
-            scores = dot_nt(kv[0, :keys], wk[place, 0, j])
-            spot = lax.broadcasted_iota(jnp.int32, (keys - prefix_len, CHUNK), 0)
-            scores = jnp.concatenate(
-                [
-                    scores[:prefix_len],
-                    jnp.where(spot <= limit, scores[prefix_len:], -jnp.inf),
-                ],
-                0,
-            )
+        def prefix_chunk(j, carry):
+            held = [slot * per_step + j for slot in slots_of[level]]
+            scores = dot_nt(kv[0, :prefix_len], wk[place, 0, j])
             top = jnp.max(scores, 0, keepdims=True)
+            for i in held:
+                top = jnp.maximum(top, stat[0, i])
             e = jnp.exp2((scores - top) * soft)
-            inv = 1.0 / jnp.sum(e, 0, keepdims=True)
-            gw = dot_nt(kv[1, :keys], wk[place, 1, j])
+            gw = dot_nt(kv[1, :prefix_len], wk[place, 1, j])
+            total = jnp.sum(e, 0, keepdims=True)
+            inner = jnp.sum(e * gw, 0, keepdims=True)
+            factors = [jnp.exp2((stat[0, i] - top) * soft) for i in held]
+            for i, factor in zip(held, factors):
+                total = total + factor * stat[1, i]
+                inner = inner + factor * stat[2, i]
+            inv = 1.0 / total
+            inner = inner * inv
+            for i, factor in zip(held, factors):
+                stat[3, i] = factor * inv
+                stat[4, i] = inner
             weights = e * inv
-            inner = jnp.sum(weights * gw, 0, keepdims=True)
-            pt[level * per_step + j, :keys] = weights.astype(BF16)
-            dt[level * per_step + j, :keys] = (weights * (gw - inner)).astype(BF16)
+            pt[level * per_step + j] = weights.astype(BF16)
+            dt[level * per_step + j] = (weights * (gw - inner)).astype(BF16)
             return carry
 
-        lax.fori_loop(0, per_step, rows_chunk, 0)
-
-    def totals(start, size, levels):
-        rows = slice(start, start + size)
+        lax.fori_loop(0, per_step, prefix_chunk, 0)
+
+    def totals(weights, grads, items):
         k_sum = v_sum = None
-        for level in levels:
-            for j in range(per_step):
-                i = level * per_step + j
-                k_part = dot_nn(dt[i, rows, :], wk[place_of[level], 0, j])
-                v_part = dot_nn(pt[i, rows, :], wk[place_of[level], 1, j])
-                k_sum = k_part if k_sum is None else k_sum + k_part
-                v_sum = v_part if v_sum is None else v_sum + v_part
+        for i, rows, place, j in items:
+            k_part = dot_nn(grads[i, rows, :], wk[place, 0, j])
+            v_part = dot_nn(weights[i, rows, :], wk[place, 1, j])
+            k_sum = k_part if k_sum is None else k_sum + k_part
+            v_sum = v_part if v_sum is None else v_sum + v_part
         return k_sum * scale, v_sum
 
     per = 256 // shard
     count = chips // per
+    base = me // per + 1
     sums = []
     for n in range(count):
-        k_sum, v_sum = totals(n * 256, 256, (0, 1))
+        chunk = lax.rem(base + n, count)
+        rows = pl.ds(pl.multiple_of(chunk * 256, 256), 256)
+        k_sum, v_sum = totals(
+            pt,
+            dt,
+            [
+                (level * per_step + j, rows, place_of[level], j)
+                for level in range(2)
+                for j in range(per_step)
+            ],
+        )
+        span = pl.ds(chunk * per, per)
         for which, value in ((0, k_sum), (1, v_sum)):
             value = value.reshape(per, 2, half, 128)
             for c in range(2):
-                tb[c, n * per : (n + 1) * per, which] = value[:, c]
-        span = pl.ds(n * per, per)
+                tb[c, span, which] = value[:, c]
         copy = remote(tb.at[1 - core, span], rb.at[span], sum_send.at[n], sum_recv.at[n], partner)
         copy.start()
         sums.append(copy)
 
-    outs = []
-
     def send_out(n):
         sums[n].wait_recv()
-        span = slice(n * per, (n + 1) * per)
+        chunk = lax.rem(base + n, count)
+        span = pl.ds(chunk * per, per)
         s2[span] = (tb[core, span] + rb[span]).astype(BF16)
         for i in range(per):
-            to = n * per + i
+            to = chunk * per + i
 
             @pl.when(to != me)
             def _():
@@ -207,24 +239,38 @@
                     s2.at[to], r2.at[me], out_send.at[to], out_recv.at[me], {"prompt": to}
                 ).start()
 
-    for c in range(2):
-        k_sum, v_sum = totals(prefix_len + c * own_keys, own_keys, (0, 1) if c == 0 else (1,))
-        rt[c, 0] = k_sum
-        rt[c, 1] = v_sum
-        if c < count - 1:
-            send_out(c)
+    def reply_chunk(i, carry):
+        weights = er[i] * stat[3, i]
+        pr[i] = weights.astype(BF16)
+        dr[i] = (weights * (gr[i] - stat[4, i])).astype(BF16)
+        return carry
+
+    lax.fori_loop(0, 3 * per_step, reply_chunk, 0)
+    for n in range(count):
+        send_out(n)
+    for c, held in ((0, ((0, 0), (1, 1))), (1, ((2, 1),))):
+        rt[c, 0], rt[c, 1] = totals(
+            pr,
+            dr,
+            [
+                (slot * per_step + j, slice(None), place_of[level], j)
+                for slot, level in held
+                for j in range(per_step)
+            ],
+        )
     pair_r = remote(rt.at[1 - core], rr, pair_send.at[2], pair_recv.at[2], partner)
     pair_r.start()
-    for n in range(min(2, count - 1), count):
-        send_out(n)
 
     kt[...] = kv[0].astype(F32).T.astype(BF16)
     for level in range(2):
-        keys = keys_of[level]
         place = place_of[level]
 
         def grads_chunk(j, carry):
-            gq = (dot_nn(kt[:, :keys], dt[level * per_step + j, :keys]) * scale).T
+            gq = dot_nn(kt[:, :prefix_len], dt[level * per_step + j])
+            for part, slot in enumerate(slots_of[level]):
+                start = prefix_len + part * own_keys
+                gq += dot_nn(kt[:, start : start + own_keys], dr[slot * per_step + j])
+            gq = (gq * scale).T
             for i in range(CHUNK // RBLK):
                 lanes = pl.multiple_of((j * (CHUNK // RBLK) + i) * 128, 128)
                 dq[place, :, pl.ds(lanes, 128)] = gq[i * RBLK : (i + 1) * RBLK]
@@ -306,8 +352,13 @@
                 vm((2, 2, per_step, CHUNK, head), BF16),
                 vm((2, keys, head), BF16),
                 vm((head, keys), BF16),
-                vm((2 * per_step, keys, CHUNK), BF16),
-                vm((2 * per_step, keys, CHUNK), BF16),
+                vm((2 * per_step, chips * shard, CHUNK), BF16),
+                vm((2 * per_step, chips * shard, CHUNK), BF16),
+                vm((3 * per_step, own_keys, CHUNK), BF16),
+                vm((3 * per_step, own_keys, CHUNK), BF16),
+                vm((3 * per_step, own_keys, CHUNK), F32),
+                vm((3 * per_step, own_keys, CHUNK), F32),
+                vm((5, 3 * per_step, 1, CHUNK), F32),
                 vm((2, chips, 2, half, head), F32),
                 vm((chips, 2, half, head), F32),
                 vm((chips, 2, half, head), BF16),

time: 29.9 us -> 27.6 us (0.923)
  Pallas kernels: 28.3 us -> 26.2 us
    pallas_call x1, Pallas kernels: 26.5 us -> 24.4 us  [local(): pl.pallas_call(functools.partial(kernel, chips, heads, per_step), out_sha...]
where the time goes in v4:
time: 27.6 us; the launch traced here: 27.5 us
  Pallas kernels  26.2 us (95%)
  between operations  1.29 us (5%)
    pallas_call x1, Pallas kernels, local(): pl.pallas_call(functools.partial(kernel, chips, heads, per_step), out_sha...  24.4 us
    pallas_call x1, Pallas kernels, local(): pl.pallas_call(finish, out_shape=tuple((jax.ShapeDtypeStruct(shape, F32)...  1.79 us

profile of v4, /device:TPU:0, one launch (start us, length us, event | category | flops | bytes accessed | tf_op | source)
XLA Modules:
  0.0 27.5 jit_solution(10197966982647820679)
XLA Ops:
  1.3 24.4 %shard_map.119 = (f32[2,128,1024]{2,1,0:T(8,128)S(1)}, f32[32,128]{1,0:T(8,128)S(1)}, f32[32,128]{1,0:T(8,128)S(1)}, f32[1,256,128]{2,1,0:T(8,128)S(1)}, f32[1,256,128]{2,1,0:T(8,128)S(1)}) custom-call(s32[1]{0:T(128)S(6)} %copy.13.len_ref, s32[1,2]{1,0:T(1,128)} %plan_ref.3, bf16[2,128,1024]{2,1,0:T(8,128)(2,1)} %bitcast.2, bf16[2,128,1024]{2,1,0:T(8,128)(2,1)} %bitcast.3, ...), custom_call_target="tpu_custom_call" | custom-call | tf_op jit(solution)/shard_map/pallas_call | solution.py:344
  25.7 1.8 %shard_map.120 = (f32[1,256,1024]{2,1,0:T(8,128)}, f32[32,128]{1,0:T(8,128)}, f32[32,128]{1,0:T(8,128)}, f32[1,256,128]{2,1,0:T(8,128)}, f32[1,256,128]{2,1,0:T(8,128)}) custom-call(s32[1,2]{1,0:T(1,128)} %plan_ref.3, f32[2,128,1024]{2,1,0:T(8,128)S(1)} %get-tuple-element.10.dq, f32[32,128]{1,0:T(8,128)S(1)} %get-tuple-element.11.pk, ...), custom_call_target="tpu_custom_call" | custom-call | tf_op jit(solution)/shard_map/pallas_call | solution.py:395

commit v5 on v4

--- a/solution.py
+++ b/solution.py
@@ -118,7 +118,7 @@
             stat[2, i] = jnp.sum(e * gw, 0, keepdims=True)
             return carry
 
-        lax.fori_loop(0, per_step, rows_chunk, 0)
+        lax.fori_loop(0, per_step, rows_chunk, 0, unroll=True)
 
     stack(sent_local, sent_block, sb)
     stack(own_local, own_block, wk.at[0])
@@ -189,7 +189,7 @@
             dt[level * per_step + j] = (weights * (gw - inner)).astype(BF16)
             return carry
 
-        lax.fori_loop(0, per_step, prefix_chunk, 0)
+        lax.fori_loop(0, per_step, prefix_chunk, 0, unroll=True)
 
     def totals(weights, grads, items):
         k_sum = v_sum = None
@@ -245,7 +245,7 @@
         dr[i] = (weights * (gr[i] - stat[4, i])).astype(BF16)
         return carry
 
-    lax.fori_loop(0, 3 * per_step, reply_chunk, 0)
+    lax.fori_loop(0, 3 * per_step, reply_chunk, 0, unroll=per_step)
     for n in range(count):
         send_out(n)
     for c, held in ((0, ((0, 0), (1, 1))), (1, ((2, 1),))):
@@ -276,7 +276,7 @@
                 dq[place, :, pl.ds(lanes, 128)] = gq[i * RBLK : (i + 1) * RBLK]
             return carry
 
-        lax.fori_loop(0, per_step, grads_chunk, 0)
+        lax.fori_loop(0, per_step, grads_chunk, 0, unroll=True)
 
     pair_r.wait_recv()
     rk_out[0] = rt[core, 0] + rr[0]

time: 27.6 us -> 25.6 us (0.928)
  Pallas kernels: 26.2 us -> 24.2 us
    pallas_call x1, Pallas kernels: 24.4 us -> 22.4 us  [local(): pl.pallas_call(functools.partial(kernel, chips, heads, per_step), out_sha...]
where the time goes in v5:
time: 25.6 us; the launch traced here: 25.5 us
  Pallas kernels  24.2 us (95%)
  between operations  1.29 us (5%)
    pallas_call x1, Pallas kernels, local(): pl.pallas_call(functools.partial(kernel, chips, heads, per_step), out_sha...  22.4 us
    pallas_call x1, Pallas kernels, local(): pl.pallas_call(finish, out_shape=tuple((jax.ShapeDtypeStruct(shape, F32)...  1.79 us

profile of v5, /device:TPU:0, one launch (start us, length us, event | category | flops | bytes accessed | tf_op | source)
XLA Modules:
  0.0 25.5 jit_solution(4451047552077877408)
XLA Ops:
  1.3 22.4 %shard_map.119 = (f32[2,128,1024]{2,1,0:T(8,128)S(1)}, f32[32,128]{1,0:T(8,128)S(1)}, f32[32,128]{1,0:T(8,128)S(1)}, f32[1,256,128]{2,1,0:T(8,128)S(1)}, f32[1,256,128]{2,1,0:T(8,128)S(1)}) custom-call(s32[1]{0:T(128)S(6)} %copy.13.len_ref, s32[1,2]{1,0:T(1,128)} %plan_ref.3, bf16[2,128,1024]{2,1,0:T(8,128)(2,1)} %bitcast.2, bf16[2,128,1024]{2,1,0:T(8,128)(2,1)} %bitcast.3, ...), custom_call_target="tpu_custom_call" | custom-call | tf_op jit(solution)/shard_map/pallas_call | solution.py:344
  23.7 1.8 %shard_map.120 = (f32[1,256,1024]{2,1,0:T(8,128)}, f32[32,128]{1,0:T(8,128)}, f32[32,128]{1,0:T(8,128)}, f32[1,256,128]{2,1,0:T(8,128)}, f32[1,256,128]{2,1,0:T(8,128)}) custom-call(s32[1,2]{1,0:T(1,128)} %plan_ref.3, f32[2,128,1024]{2,1,0:T(8,128)S(1)} %get-tuple-element.10.dq, f32[32,128]{1,0:T(8,128)S(1)} %get-tuple-element.11.pk, ...), custom_call_target="tpu_custom_call" | custom-call | tf_op jit(solution)/shard_map/pallas_call | solution.py:395
